TPU v7x, 128 devices: a whole 4x4x4 slice. The times are simulated.
128 devices in a mesh: req: 16 (over z, y), tp: 8 (over x, core).
Axes of the slice: x: 4, y: 4, z: 4, core: 2. Of those that a mesh axis runs over, the one named last changes fastest.
Arguments:
- hidden_in: bfloat16 [4096, 1024], P('req'), may hold values from -42 to 42
- prompt_kv: bfloat16 [2, 128, 512, 1024], P(None, 'req', None, 'tp'), may hold values from -9 to 9
- tail_kv: bfloat16 [2, 4096, 64, 1024], P(None, 'req', None, 'tp'), may hold values from -9 to 9
- group_of: int32 [4096], P('req'), may hold values from 0 to 7
- prompt_len: int32 [128], P('req'), may hold values from 64 to 512, as said below
- tail_len: int32 [4096], P('req'), may hold values from 0 to 63, as said below
- bucket_of: int32 [577], replicated, may hold values from 0 to 31, never falling along the last dimension, each value on 1 to 38 neighbouring positions
- bias_table: float32 [32, 16], P(None, 'tp'), may hold values from -6 to 302
- attn_gain: float32 [1024], replicated, may hold values from 0.1 to 1.9
- w_query: bfloat16 [1024, 1024], P(None, 'tp'), may hold values from -0.1875 to 0.1875
- w_key: bfloat16 [1024, 1024], P(None, 'tp'), may hold values from -0.1875 to 0.1875
- w_value: bfloat16 [1024, 1024], P(None, 'tp'), may hold values from -0.1875 to 0.1875
- w_out: bfloat16 [1024, 1024], P('tp'), may hold values from -0.75 to 0.75
- ffn_gain: float32 [1024], replicated, may hold values from 0.1 to 1.9
- router_weight: bfloat16 [1024, 16], replicated, may hold values from -0.1875 to 0.1875
- expert_ids: int32 [4096, 2], P('req'), may hold values from 0 to 15, all different within a row; in each aligned block of 256 rows (0 to 255, 256 to 511, ...) at most 40 rows name the same one
- w_gate: bfloat16 [16, 1024, 2816], P('req', None, 'tp'), may hold values from -0.1875 to 0.1875
- w_up: bfloat16 [16, 1024, 2816], P('req', None, 'tp'), may hold values from -0.1875 to 0.1875
- w_down: bfloat16 [16, 2816, 1024], P('req', 'tp'), may hold values from -0.109375 to 0.109375
- new_slot: int32 [4096], replicated, may hold values from 0 to 4095, as said below
Outputs:
- out_hidden: bfloat16 [4096, 1024], P('req')
- new_tail_kv: bfloat16 [2, 4096, 64, 1024], P(None, 'req', None, 'tp')
Inputs may be any that keep to these rules, and one draw needn't show every extreme that they name: `expert_ids`: in each replica's aligned block of 256 tokens no expert is named by more than 40 of them, a bound that some block reaches. `new_slot`: A permutation. Exactly 4 requests of each replica are movers; all movers of one replica go to one replica (possibly itself), each taking a slot that a mover of that replica leaves; every other request keeps its slot. `prompt_len`: each replica has a group of 512 rows. `tail_len`: each replica has a request of 63 own rows and one of none.
All inputs are finite; a program needn't handle non-finite values.
Results may differ from a plain program's by a relative error of at most 0.013.
Values may be sent and summed in bfloat16 or wider, within the bound.
A program may use at most 128 MiB of HBM per device.

v0:
```python
import jax
import jax.numpy as jnp
from jax import lax
from jax.sharding import PartitionSpec as P

HD = 64
TOP = 2
MIG = 4
EPS = 1e-06


def rms_scale(values, gain):
    v = values.astype(jnp.float32)
    return (v * lax.rsqrt(jnp.mean(v * v, axis=-1, keepdims=True) + EPS) * gain).astype(
        jnp.bfloat16
    )


def bias_lookup(distance, starts, finish, bias_table):
    within = (distance[..., None] >= starts) & (distance[..., None] < finish)
    return jnp.einsum(
        "rjk,kh->hrj", within.astype(jnp.float32), bias_table, precision=lax.Precision.HIGHEST
    )


def attention(
    hidden_in,
    prompt_kv,
    tail_kv,
    group_of,
    prompt_len,
    tail_len,
    bucket_of,
    bias_table,
    attn_gain,
    w_query,
    w_key,
    w_value,
):
    normed = rms_scale(hidden_in, attn_gain)
    query = jnp.dot(normed, w_query, preferred_element_type=jnp.float32).astype(jnp.bfloat16)
    key_new = jnp.dot(normed, w_key, preferred_element_type=jnp.float32).astype(jnp.bfloat16)
    value_new = jnp.dot(normed, w_value, preferred_element_type=jnp.float32).astype(jnp.bfloat16)
    rows = hidden_in.shape[0]
    heads_here = w_query.shape[1] // HD
    groups_here = prompt_kv.shape[1]
    prompt_rows = prompt_kv.shape[2]
    tail_rows = tail_kv.shape[2]
    span = bucket_of.shape[0]
    buckets = bias_table.shape[0]
    bucket_ids = jnp.arange(buckets, dtype=jnp.int32)
    starts = jnp.sum((bucket_of[:, None] < bucket_ids[None, :]).astype(jnp.int32), axis=0)
    finish = jnp.concatenate([starts[1:], jnp.full((1,), span, jnp.int32)])
    first_bias = jnp.sum(jnp.where((bucket_ids == bucket_of[0])[:, None], bias_table, 0.0), axis=0)
    scale = HD ** (-0.5)
    q = query.reshape(rows, heads_here, HD)
    pk = prompt_kv[0].reshape(groups_here, prompt_rows, heads_here, HD)
    pv = prompt_kv[1].reshape(groups_here, prompt_rows, heads_here, HD)
    tk = tail_kv[0].reshape(rows, tail_rows, heads_here, HD)
    tv = tail_kv[1].reshape(rows, tail_rows, heads_here, HD)
    kn = key_new.reshape(rows, heads_here, HD)
    vn = value_new.reshape(rows, heads_here, HD)
    group_hit = group_of[:, None] == jnp.arange(groups_here, dtype=jnp.int32)[None, :]
    own_len = jnp.sum(jnp.where(group_hit, prompt_len[None, :], 0), axis=1)
    pos = own_len + tail_len
    jpos = jnp.arange(prompt_rows, dtype=jnp.int32)
    pidx = jnp.clip(pos[:, None] - jpos[None, :], 0, span - 1)
    pbias = bias_lookup(pidx, starts, finish, bias_table)
    pmask = group_hit[:, :, None] & (jpos[None, None, :] < own_len[:, None, None])
    ps = (
        jnp.einsum("rhd,gjhd->hrgj", q, pk, preferred_element_type=jnp.float32) * scale
        + pbias[:, :, None, :]
    )
    ps = jnp.where(pmask[None], ps, -jnp.inf)
    tpos = jnp.arange(tail_rows, dtype=jnp.int32)
    tidx = jnp.clip(tail_len[:, None] - tpos[None, :], 0, span - 1)
    tbias = bias_lookup(tidx, starts, finish, bias_table)
    tmask = tpos[None, :] < tail_len[:, None]
    ts = jnp.einsum("rhd,rthd->hrt", q, tk, preferred_element_type=jnp.float32) * scale + tbias
    ts = jnp.where(tmask[None], ts, -jnp.inf)
    ns = (
        jnp.einsum("rhd,rhd->hr", q, kn, preferred_element_type=jnp.float32) * scale
        + first_bias[:, None]
    )
    top = jnp.maximum(jnp.maximum(jnp.max(ps, axis=(2, 3)), jnp.max(ts, axis=2)), ns)
    pe = jnp.exp(ps - top[:, :, None, None])
    te = jnp.exp(ts - top[:, :, None])
    ne = jnp.exp(ns - top)
    total = jnp.sum(pe, axis=(2, 3)) + jnp.sum(te, axis=2) + ne
    pw = (pe / total[:, :, None, None]).astype(jnp.bfloat16)
    tw = (te / total[:, :, None]).astype(jnp.bfloat16)
    nw = (ne / total).astype(jnp.bfloat16)
    head = jnp.einsum("hrgj,gjhd->rhd", pw, pv, preferred_element_type=jnp.float32)
    head = head + jnp.einsum("hrt,rthd->rhd", tw, tv, preferred_element_type=jnp.float32)
    head = head + jnp.einsum("hr,rhd->rhd", nw, vn, preferred_element_type=jnp.float32)
    head_out = head.reshape(rows, heads_here * HD).astype(jnp.bfloat16)
    return (head_out, key_new, value_new, tmask)


def body(
    hidden_in,
    prompt_kv,
    tail_kv,
    group_of,
    prompt_len,
    tail_len,
    bucket_of,
    bias_table,
    attn_gain,
    w_query,
    w_key,
    w_value,
    w_out,
    ffn_gain,
    router_weight,
    expert_ids,
    w_gate,
    w_up,
    w_down,
    new_slot,
):
    head_out, key_new, value_new, tmask = attention(
        hidden_in,
        prompt_kv,
        tail_kv,
        group_of,
        prompt_len,
        tail_len,
        bucket_of,
        bias_table,
        attn_gain,
        w_query,
        w_key,
        w_value,
    )
    rows = hidden_in.shape[0]
    width = hidden_in.shape[1]
    local_idx = jnp.arange(rows, dtype=jnp.int32)
    tail_rows = tail_kv.shape[2]
    write_row = jnp.arange(tail_rows, dtype=jnp.int32)[None, :] == tail_len[:, None]
    fresh = jnp.stack([key_new, value_new])[:, :, None, :]
    tail_new = jnp.where(write_row[None, :, :, None], fresh, tail_kv)
    partial_attn = jnp.dot(head_out, w_out, preferred_element_type=jnp.float32)
    attn = lax.psum(partial_attn, "tp")
    resid = (hidden_in.astype(jnp.float32) + attn).astype(jnp.bfloat16)
    normed2 = rms_scale(resid, ffn_gain)
    logits = jnp.dot(normed2, router_weight, preferred_element_type=jnp.float32)
    experts = router_weight.shape[1]
    expert_range = jnp.arange(experts, dtype=jnp.int32)
    first_hit = expert_ids[:, 0:1] == expert_range[None, :]
    second_hit = expert_ids[:, 1:2] == expert_range[None, :]
    picked_first = jnp.sum(jnp.where(first_hit, logits, 0.0), axis=1)
    picked_second = jnp.sum(jnp.where(second_hit, logits, 0.0), axis=1)
    gate_first = jax.nn.sigmoid(picked_first - picked_second)
    capacity = 5 * rows * TOP // (4 * experts)
    flat_e = expert_ids.reshape(-1)
    onehot = (flat_e[:, None] == expert_range[None, :]).astype(jnp.int32)
    slot_pos = jnp.sum((jnp.cumsum(onehot, axis=0) - 1) * onehot, axis=1)
    target = flat_e * capacity + slot_pos
    placed = (target[:, None] == jnp.arange(experts * capacity, dtype=jnp.int32)[None, :]).astype(
        jnp.bfloat16
    )
    doubled = jnp.repeat(normed2, TOP, axis=0)
    outgoing = (
        jnp.dot(placed.T, doubled, preferred_element_type=jnp.float32)
        .astype(jnp.bfloat16)
        .reshape(experts, capacity, width)
    )
    gate_mat = w_gate[0]
    up_mat = w_up[0]
    down_mat = w_down[0]
    received = lax.all_to_all(outgoing, "req", split_axis=0, concat_axis=0, tiled=True)
    flat = received.reshape(-1, received.shape[-1])
    gate_h = jnp.dot(flat, gate_mat, preferred_element_type=jnp.float32)
    up_h = jnp.dot(flat, up_mat, preferred_element_type=jnp.float32)
    act = (jax.nn.gelu(gate_h, approximate=True) * up_h).astype(jnp.bfloat16)
    summed = lax.psum(
        jnp.dot(act, down_mat, preferred_element_type=jnp.float32).astype(jnp.bfloat16), "tp"
    )
    back = summed.reshape(received.shape)
    result = lax.all_to_all(back, "req", split_axis=0, concat_axis=0, tiled=True)
    pair_out = jnp.dot(
        placed, result.reshape(experts * capacity, width), preferred_element_type=jnp.float32
    ).reshape(rows, TOP, width)
    mixed = (
        resid.astype(jnp.float32)
        + gate_first[:, None] * pair_out[:, 0]
        + (1.0 - gate_first)[:, None] * pair_out[:, 1]
    ).astype(jnp.bfloat16)
    replicas = lax.axis_size("req")
    me = lax.axis_index("req")
    total_reqs = new_slot.shape[0]
    everyone = jnp.arange(total_reqs, dtype=jnp.int32)
    leaving_all = new_slot // rows != everyone // rows
    rank_all = (
        jnp.cumsum(leaving_all.reshape(replicas, rows).astype(jnp.int32), axis=1) - 1
    ).reshape(-1)
    source_of = jnp.zeros((total_reqs,), jnp.int32).at[new_slot].set(everyone)
    first_slot = me * rows
    leaving = lax.dynamic_slice_in_dim(leaving_all, first_slot, rows, 0)
    my_rank = lax.dynamic_slice_in_dim(rank_all, first_slot, rows, 0)
    send_idx = (
        jnp.zeros((MIG,), jnp.int32)
        .at[jnp.where(leaving, my_rank, MIG)]
        .set(local_idx, mode="drop")
    )
    send_rows = mixed[send_idx]
    send_tail = jnp.swapaxes(tail_new[:, send_idx], 0, 1)
    got_rows, got_tail = (
        lax.all_gather(send_rows, "req", axis=0, tiled=True),
        lax.all_gather(send_tail, "req", axis=0, tiled=True),
    )
    count = jnp.sum(leaving.astype(jnp.int32))
    vacated = jnp.where(jnp.arange(MIG, dtype=jnp.int32) < count, send_idx, rows)
    source = source_of[first_slot + jnp.minimum(vacated, rows - 1)]
    position = source // rows * MIG + rank_all[source]
    position = jnp.clip(position, 0, got_rows.shape[0] - 1)
    out_hidden = mixed.at[vacated].set(got_rows[position], mode="drop")
    new_tail_kv = tail_new.at[:, vacated].set(jnp.swapaxes(got_tail[position], 0, 1), mode="drop")
    return (out_hidden, new_tail_kv)


def solution(mesh):
    return jax.shard_map(
        body,
        mesh=mesh,
        in_specs=(
            P("req", None),
            P(None, "req", None, "tp"),
            P(None, "req", None, "tp"),
            P("req"),
            P("req"),
            P("req"),
            P(),
            P(None, "tp"),
            P(),
            P(None, "tp"),
            P(None, "tp"),
            P(None, "tp"),
            P("tp", None),
            P(),
            P(),
            P("req", None),
            P("req", None, "tp"),
            P("req", None, "tp"),
            P("req", "tp", None),
            P(),
        ),
        out_specs=(P("req", None), P(None, "req", None, "tp")),
        check_vma=False,
    )
```

profile of v0, /device:TPU:6, one launch (start us, length us, event | category | flops | bytes accessed | tf_op | source)
XLA Modules:
  0.0 309.5 jit_solution(10653071250375701447)
XLA Ops:
  15.9 6.9 %fusion.8 = f32[2,256,512]{2,0,1:T(2,128)S(1)} fusion(s32[256,512]{1,0:T(8,128)S(1)} %subtract_clamp_fusion, s32[32]{0:T(128)S(1)} %pad_add_fusion, s32[32]{0:T(128)S(1)} %convert_reduce_fusion, f32[32,2]{0,1:T(2,128)} %param.27), kind=kOutput, calls=%fused_computation.35 | convolution fusion | flops 113246208 | bytes 1573376 | tf_op jit(solution)/shard_map/rjk,kh->hrj/dot_general | solution.py:21
  25.8 6.5 %fusion.89 = (bf16[1,256,64,128]{3,2,1,0:T(8,128)(2,1)}, bf16[1,256,64,128]{3,2,1,0:T(8,128)(2,1)}) fusion(bf16[2,256,64,128]{3,2,1,0:T(8,128)(2,1)} %param.22), kind=kLoop, calls=%fused_computation.187 | loop fusion | bytes 16777216 | tf_op jit(solution)/shard_map/slice | solution.py:59
  32.3 7.0 %copy.114 = bf16[1,256,64,128]{1,3,2,0:T(8,128)(2,1)} copy(bf16[1,256,64,128]{3,2,1,0:T(8,128)(2,1)} %get-tuple-element.12) | data formatting | bytes 8388608
  42.9 3.7 %multiply_reduce_fusion.1 = f32[2,256,64]{1,0,2:T(2,128)S(1)} fusion(bf16[2,256,64,64]{1,2,0,3:T(8,128)(2,1)} %bitcast.145, f32[2,256,64]{1,2,0:T(8,128)S(1)} %get-tuple-element.27), kind=kLoop, calls=%fused_computation.13 | loop fusion | flops 6258688 | bytes 4456448 | tf_op jit(solution)/shard_map/rhd,rthd->hrt/dot_general | solution.py:79
  47.6 2.2 fusion.5
  49.9 2.7 fusion.4
  54.7 6.9 %copy.116 = bf16[1,256,64,128]{1,3,2,0:T(8,128)(2,1)} copy(bf16[1,256,64,128]{3,2,1,0:T(8,128)(2,1)} %get-tuple-element.13) | data formatting | bytes 8388608
  63.6 2.3 copy.115
  65.9 3.2 %multiply_reduce_fusion = f32[256,2,64]{0,2,1:T(8,128)S(1)} fusion(bf16[256,2,64,64]{0,3,1,2:T(8,128)(2,1)} %bitcast.146, f32[256,2,64]{0,1,2:T(2,128)S(1)} %bitcast_convert_fusion), kind=kLoop, calls=%fused_computation.12 | loop fusion | flops 6258688 | bytes 4456448 | tf_op jit(solution)/shard_map/hrt,rthd->rhd/dot_general | solution.py:94
  69.2 5.1 %fusion.19 = bf16[256,2,64]{0,2,1:T(8,128)(2,1)S(1)} fusion(f32[256,2,64]{0,2,1:T(8,128)S(1)} %multiply_reduce_fusion, f32[2,256,8,512]{3,1,2,0:T(8,128)} %copy-done.1, f32[2,256]{1,0:T(2,128)S(1)} %copy-done.18, f32[2,256]{1,0:T(2,128)S(1)} %copy-done.13, f32[2,256,512]{2,1,0:T(8,128)S(1)} %copy.78, pred[256,8,512]{2,0,1:T(8,128)(4,1)S(1)} %broadcast_and_fusion, ...), kind=kOutput, calls=%fused_computation.52 | convolution fusion | flops 281182208 | bytes 11802624 | tf_op jit(solution)/shard_map/hrgj,gjhd->rhd/dot_general | solution.py:93
  77.6 60.5 %all-reduce.3.cloned.1.call-done = f32[256,1024]{1,0:T(8,128)} async-done(((f32[256,1024]{1,0:T(8,128)}), f32[256,1024]{1,0:T(8,128)}) %all-reduce.3.cloned.1.call-update) | async-done | bytes 1048592 | tf_op jit(solution)/shard_map/psum | solution.py:144
  141.6 3.2 %convolution_convert_fusion.1 = bf16[640,1024]{1,0:T(8,128)(2,1)} fusion(bf16[512,1024]{1,0:T(8,128)(2,1)} %reshape.353, s32[512]{0:T(512)S(1)} %multiply_add_fusion), kind=kOutput, calls=%fused_computation.28 | convolution fusion | flops 672071680 | bytes 2361344 | tf_op jit(solution)/shard_map/dot_general | solution.py:165
  144.9 7.0 %all-to-all-start = ((bf16[16,40,1024]{2,1,0:T(8,128)(2,1)}), bf16[16,40,1024]{2,1,0:T(8,128)(2,1)S(1)}, u32[]{:S(2)}, u32[]{:S(2)}) async-start(bf16[16,40,1024]{2,1,0:T(8,128)(2,1)} %bitcast.149), calls=%async_computation | async-start | bytes 2621440 | tf_op jit(solution)/shard_map/all_to_all | solution.py:172
  156.0 20.2 %all-to-all-done = bf16[16,40,1024]{2,1,0:T(8,128)(2,1)S(1)} async-done(((bf16[16,40,1024]{2,1,0:T(8,128)(2,1)}), bf16[16,40,1024]{2,1,0:T(8,128)(2,1)S(1)}, u32[]{:S(2)}, u32[]{:S(2)}) %all-to-all-start) | async-done | bytes 1310752 | tf_op jit(solution)/shard_map/all_to_all | solution.py:172
  176.1 2.8 fusion.48
  178.9 4.3 %convolution_convert_fusion = bf16[640,1024]{1,0:T(8,128)(2,1)} fusion(bf16[640,1024]{1,0:T(8,128)(2,1)S(1)} %bitcast.148, f32[640,352]{0,1:T(8,128)} %fusion.48, bf16[1,352,1024]{2,1,0:T(8,128)(2,1)S(1)} %copy-done, bf16[1,1024,352]{1,2,0:T(8,128)(2,1)} %param.37), kind=kOutput, calls=%fused_computation.27 | convolution fusion | flops 925655040 | bytes 4964352 | tf_op jit(solution)/shard_map/dot_general | solution.py:178
  183.3 8.3 %broadcast_select_fusion = bf16[2,256,64,128]{3,2,1,0:T(8,128)(2,1)} fusion(bf16[2,256,64,128]{3,2,1,0:T(8,128)(2,1)} %param.22, pred[256,64]{1,0:T(8,128)(4,1)S(1)} %copy.89, bf16[2,256,128]{2,1,0:T(8,128)(2,1)S(1)} %copy.90), kind=kLoop, calls=%fused_computation.20 | loop fusion | flops 4194304 | bytes 16924672 | tf_op jit(solution)/shard_map/jit(_where)/select_n | solution.py:142
  191.5 4.7 %gather_fusion.3 = bf16[4,2,64,128]{3,2,1,0:T(8,128)(2,1)} fusion(bf16[2,256,64,128]{3,2,1,0:T(8,128)(2,1)} %broadcast_select_fusion, s32[1024]{0:T(1024)S(1)} %pad_clamp_fusion.3), kind=kCustom, calls=%fused_computation.4 | custom fusion | bytes 262160 | tf_op jit(solution)/shard_map/gather | solution.py:208
  196.5 15.5 %scatter_custom_fusion.1 = s32[4096]{0:T(1024)S(1)} fusion(s32[4096]{0:T(1024)S(1)} %add_select_fusion.1, s32[4096]{0:T(1024)S(1)} %iota.80, s32[]{:T(128)} %constant.36.clone.1), kind=kCustom, calls=%fused_computation.136 | custom fusion | bytes 16388 | tf_op jit(solution)/shard_map/scatter | solution.py:198
  212.7 28.9 %all-reduce.5.cloned.1.call-done = bf16[16,40,1024]{2,1,0:T(8,128)(2,1)} async-done(((bf16[16,40,1024]{2,1,0:T(8,128)(2,1)}), bf16[16,40,1024]{2,1,0:T(8,128)(2,1)}) %all-reduce.5.cloned.1.call-update) | async-done | bytes 1310736 | tf_op jit(solution)/shard_map/psum | solution.py:177
  241.6 7.0 %all-to-all-start.1 = ((bf16[16,40,1024]{2,1,0:T(8,128)(2,1)}), bf16[16,40,1024]{2,1,0:T(8,128)(2,1)S(1)}, u32[]{:S(2)}, u32[]{:S(2)}) async-start(bf16[16,40,1024]{2,1,0:T(8,128)(2,1)} %all-reduce.5.cloned.1.call-done), calls=%async_computation.1 | async-start | bytes 2621440 | tf_op jit(solution)/shard_map/all_to_all | solution.py:181
  249.6 23.0 %all-to-all-done.1 = bf16[16,40,1024]{2,1,0:T(8,128)(2,1)S(1)} async-done(((bf16[16,40,1024]{2,1,0:T(8,128)(2,1)}), bf16[16,40,1024]{2,1,0:T(8,128)(2,1)S(1)}, u32[]{:S(2)}, u32[]{:S(2)}) %all-to-all-start.1) | async-done | bytes 1310752 | tf_op jit(solution)/shard_map/all_to_all | solution.py:181
  274.5 22.0 %all-gather.1 = bf16[16,4,1024]{2,1,0:T(4,128)(2,1)S(1)} all-gather(bf16[1,4,1024]{2,1,0:T(4,128)(2,1)S(1)} %bitcast.160), channel_id=2, replica_groups=mesh['req'=16,'tp'=8] {'req'}, dimensions={0}, use_global_device_ids=true | all-gather | bytes 139264 | tf_op jit(solution)/shard_map/all_gather | solution.py:210
  297.7 2.3 gather_fusion.4
  (150 shorter events, 36.9 us)
Async XLA Ops:
  8.0 170.9 %copy-start = (bf16[1,352,1024]{2,1,0:T(8,128)(2,1)S(1)}, bf16[1,352,1024]{2,1,0:T(8,128)(2,1)}, u32[]{:S(2)}) copy-start(bf16[1,352,1024]{2,1,0:T(8,128)(2,1)} %param.38) | copy-start | bytes 2162692
  8.0 130.1 %all-reduce.3.cloned.1.call-start = ((), (), s32[]{:S(2)}) async-start(), calls=%async_computation.2 | async-start | bytes 2097152 | tf_op jit(solution)/shard_map/psum | solution.py:144
  14.4 8.4 %copy-start.24 = (s32[32]{0:T(128)}, s32[32]{0:T(128)S(1)}, u32[]{:S(2)}) copy-start(s32[32]{0:T(128)S(1)} %convert_reduce_fusion) | copy-start | bytes 388
  15.9 6.9 %copy-start.29 = (s32[32]{0:T(128)}, s32[32]{0:T(128)S(1)}, u32[]{:S(2)}) copy-start(s32[32]{0:T(128)S(1)} %pad_add_fusion) | copy-start | bytes 388
  15.9 7.1 %copy-start.3 = (bf16[256,1024]{1,0:T(8,128)(2,1)S(1)}, bf16[256,1024]{1,0:T(8,128)(2,1)}, u32[]{:S(2)}) copy-start(bf16[256,1024]{1,0:T(8,128)(2,1)} %param.20) | copy-start | bytes 1572868
  15.9 7.3 %copy-start.2 = (bf16[2,8,512,128]{3,2,1,0:T(8,128)(2,1)S(1)}, bf16[2,8,512,128]{3,2,1,0:T(8,128)(2,1)}, u32[]{:S(2)}) copy-start(bf16[2,8,512,128]{3,2,1,0:T(8,128)(2,1)} %param.21) | copy-start | bytes 6291460
  23.2 16.1 %copy-start.23 = (f32[256]{0:T(256)}, f32[256]{0:T(256)S(1)}, u32[]{:S(2)}) copy-start(f32[256]{0:T(256)S(1)} %add_rsqrt_fusion.1) | copy-start | bytes 3076
  32.3 7.0 %copy-start.26 = (bf16[1024,128]{1,0:T(8,128)(2,1)S(1)}, bf16[1024,128]{1,0:T(8,128)(2,1)}, u32[]{:S(2)}) copy-start(bf16[1024,128]{1,0:T(8,128)(2,1)} %param.29) | copy-start | bytes 786436
  32.3 7.0 %copy-start.28 = (f32[1024]{0:T(1024)S(1)}, f32[1024]{0:T(1024)}, u32[]{:S(2)}) copy-start(f32[1024]{0:T(1024)} %param.28) | copy-start | bytes 12292
  32.3 7.5 %copy-start.27 = (bf16[1024,128]{1,0:T(8,128)(2,1)S(1)}, bf16[1024,128]{1,0:T(8,128)(2,1)}, u32[]{:S(2)}) copy-start(bf16[1024,128]{1,0:T(8,128)(2,1)} %param.30) | copy-start | bytes 786436
  32.3 9.2 %copy-start.21 = (f32[32,2]{0,1:T(2,128)S(1)}, f32[32,2]{0,1:T(2,128)}, u32[]{:S(2)}) copy-start(f32[32,2]{0,1:T(2,128)} %param.27) | copy-start | bytes 772
  39.3 7.3 %copy-start.8 = (s32[256,64]{0,1:T(8,128)S(1)}, s32[256,64]{0,1:T(8,128)}, u32[]{:S(2)}) copy-start(s32[256,64]{0,1:T(8,128)} %subtract_clamp_fusion.1) | copy-start | bytes 196612
  39.3 7.3 %copy-start.16 = (pred[256,64]{0,1:T(8,128)(4,1)S(1)}, pred[256,64]{0,1:T(8,128)(4,1)}, u32[]{:S(2)}) copy-start(pred[256,64]{0,1:T(8,128)(4,1)} %get-tuple-element.21) | copy-start | bytes 49156
  39.3 7.3 %copy-start.22 = (f32[32,2]{0,1:T(2,128)S(1)}, f32[32,2]{0,1:T(2,128)}, u32[]{:S(2)}) copy-start(f32[32,2]{0,1:T(2,128)} %param.27) | copy-start | bytes 772
  39.3 7.3 %copy-start.25 = (s32[32]{0:T(128)S(1)}, s32[32]{0:T(128)}, u32[]{:S(2)}) copy-start(s32[32]{0:T(128)} %copy-done.24) | copy-start | bytes 388
  39.4 7.3 %copy-start.30 = (s32[32]{0:T(128)S(1)}, s32[32]{0:T(128)}, u32[]{:S(2)}) copy-start(s32[32]{0:T(128)} %copy-done.29) | copy-start | bytes 388
  74.3 65.3 %copy-start.19 = (f32[1024]{0:T(1024)S(1)}, f32[1024]{0:T(1024)}, u32[]{:S(2)}) copy-start(f32[1024]{0:T(1024)} %param.33) | copy-start | bytes 12292
  140.4 11.6 %copy-start.9 = (s32[4096]{0:T(1024)S(1)}, s32[4096]{0:T(1024)}, u32[]{:S(2)}) copy-start(s32[4096]{0:T(1024)} %param.39) | copy-start | bytes 49156
  140.4 12.5 %copy-start.11 = (bf16[256,128]{0,1:T(8,128)(2,1)S(1)}, bf16[256,128]{0,1:T(8,128)(2,1)}, u32[]{:S(2)}) copy-start(bf16[256,128]{0,1:T(8,128)(2,1)} %convolution_convert_fusion.2) | copy-start | bytes 196612
  144.9 31.2 %all-to-all-start = ((bf16[16,40,1024]{2,1,0:T(8,128)(2,1)}), bf16[16,40,1024]{2,1,0:T(8,128)(2,1)S(1)}, u32[]{:S(2)}, u32[]{:S(2)}) async-start(bf16[16,40,1024]{2,1,0:T(8,128)(2,1)} %bitcast.149), calls=%async_computation | async-start | bytes 2621440 | tf_op jit(solution)/shard_map/all_to_all | solution.py:172
  151.9 89.7 %all-reduce.5.cloned.1.call-start = ((), (), s32[]{:S(2)}) async-start(), calls=%async_computation.3 | async-start | bytes 2621440 | tf_op jit(solution)/shard_map/psum | solution.py:177
  183.2 114.4 %all-gather.4.cloned.1.call-start = ((), (), s32[]{:S(2)}) async-start(), calls=%async_computation.4 | async-start | bytes 2228224 | tf_op jit(solution)/shard_map/all_gather | solution.py:211
  191.5 57.8 %copy-start.14 = (bf16[1024,16]{0,1:T(8,128)(2,1)S(1)}, bf16[1024,16]{0,1:T(8,128)(2,1)}, u32[]{:S(2)}) copy-start(bf16[1024,16]{0,1:T(8,128)(2,1)} %param.34) | copy-start | bytes 98308
  241.6 31.1 %all-to-all-start.1 = ((bf16[16,40,1024]{2,1,0:T(8,128)(2,1)}), bf16[16,40,1024]{2,1,0:T(8,128)(2,1)S(1)}, u32[]{:S(2)}, u32[]{:S(2)}) async-start(bf16[16,40,1024]{2,1,0:T(8,128)(2,1)} %all-reduce.5.cloned.1.call-done), calls=%async_computation.1 | async-start | bytes 2621440 | tf_op jit(solution)/shard_map/all_to_all | solution.py:181
  (12 other events, 47.2 us)
Sparse Core Ops, SparseCore 0:
  75.7 62.3 all-reduce.2
  183.3 58.1 all-reduce.4
Sparse Core Ops, SparseCore 1:
  196.3 42.1 all-gather.3
where the time goes:
time: 311 us; the launch traced here: 309 us
  waiting for transfers between devices  133 us (43%)
  local copies, waits for them, and re-layouts  59.9 us (19%)
  other arithmetic  33 us (11%)
  matrix products  31.5 us (10%)
  blocking collectives  22 us (7%)
  between operations  16.2 us (5%)
  starting transfers between devices  14.1 us (5%)
    psum x1, waiting for transfers between devices, body(): attn = lax.psum(partial_attn, 'tp')  60.5 us
    psum x1, waiting for transfers between devices, body(): lax.psum(jnp.dot(act, down_mat, preferred_element_type=jnp.float32).astyp...  28.9 us
    all_to_all x1, waiting for transfers between devices, body(): lax.all_to_all(back, 'req', split_axis=0, concat_axis=0, tiled=True)  23 us
    all_gather x1, blocking collectives, body(): lax.all_gather(send_rows, 'req', axis=0, tiled=True)  22 us
    all_to_all x1, waiting for transfers between devices, body(): lax.all_to_all(outgoing, 'req', split_axis=0, concat_axis=0, tiled=True)  20.2 us
    unnamed x68, local copies, waits for them, and re-layouts  18.9 us
    scatter x1, local copies, waits for them, and re-layouts, body(): source_of = jnp.zeros((total_reqs,), jnp.int32).at[new_slot].set(everyone)  15.5 us
    select_n x1, other arithmetic, body(): tail_new = jnp.where(write_row[None, :, :, None], fresh, tail_kv)  8.26 us
  transfers between devices with their start and end apart: 5, of which 4 were waited for; matrix products, arithmetic and copies ran while one was open for 13% of the time, Pallas kernels for 0%

commit v1 on v0

--- a/solution.py
+++ b/solution.py
@@ -7,6 +7,11 @@
 TOP = 2
 MIG = 4
 EPS = 1e-06
+
+
+def add_all(value, name):
+    pieces = lax.all_gather(value, name)
+    return jnp.sum(pieces, axis=0)
 
 
 def rms_scale(values, gain):
@@ -174,7 +179,7 @@
     gate_h = jnp.dot(flat, gate_mat, preferred_element_type=jnp.float32)
     up_h = jnp.dot(flat, up_mat, preferred_element_type=jnp.float32)
     act = (jax.nn.gelu(gate_h, approximate=True) * up_h).astype(jnp.bfloat16)
-    summed = lax.psum(
+    summed = add_all(
         jnp.dot(act, down_mat, preferred_element_type=jnp.float32).astype(jnp.bfloat16), "tp"
     )
     back = summed.reshape(received.shape)

time: 311 us -> 336 us (1.080)
  blocking collectives: 22 us -> 51.2 us
  other arithmetic: 33 us -> 41.1 us
  waiting for transfers between devices: 133 us -> 125 us
  starting transfers between devices: 14.1 us -> 7.34 us
    all_gather x1, waiting for transfers between devices: 0.03 us -> 44.5 us  [body(): lax.all_gather(send_tail, 'req', axis=0, tiled=True)]
    psum x1 -> x0, waiting for transfers between devices: 28.9 us -> none  [body(): lax.psum(jnp.dot(act, down_mat, preferred_element_type=jnp.float32).astyp...]
    all_to_all x0 -> x1, blocking collectives: none -> 28.2 us  [body(): lax.all_to_all(outgoing, 'req', split_axis=0, concat_axis=0, tiled=True)]
    all_to_all x1, waiting for transfers between devices: 23 us -> 0.01 us  [body(): lax.all_to_all(back, 'req', split_axis=0, concat_axis=0, tiled=True)]
    all_to_all x1 -> x0, waiting for transfers between devices: 20.2 us -> none  [body(): lax.all_to_all(outgoing, 'req', split_axis=0, concat_axis=0, tiled=True)]
    all_gather x0 -> x1, waiting for transfers between devices: none -> 19.9 us  [add_all(): pieces = lax.all_gather(value, name)]
    reduce_sum x0 -> x1, other arithmetic: none -> 8.08 us  [add_all(): return jnp.sum(pieces, axis=0)]
    all_to_all x1 -> x0, starting transfers between devices: 6.98 us -> none  [body(): lax.all_to_all(outgoing, 'req', split_axis=0, concat_axis=0, tiled=True)]
  transfers between devices with their start and end apart: 5 -> 4, of which waited for: 4 -> 3; matrix products, arithmetic and copies ran while one was open for 13% -> 15% of each run, Pallas kernels for 0% -> 0%
where the time goes in v1:
time: 336 us; the launch traced here: 335 us
  waiting for transfers between devices  125 us (37%)
  local copies, waits for them, and re-layouts  63.2 us (19%)
  blocking collectives  51.2 us (15%)
  other arithmetic  41.1 us (12%)
  matrix products  32.6 us (10%)
  between operations  14.3 us (4%)
  starting transfers between devices  7.34 us (2%)
    psum x1, waiting for transfers between devices, body(): attn = lax.psum(partial_attn, 'tp')  60.5 us
    all_gather x1, waiting for transfers between devices, body(): lax.all_gather(send_tail, 'req', axis=0, tiled=True)  44.5 us
    all_to_all x1, blocking collectives, body(): lax.all_to_all(outgoing, 'req', split_axis=0, concat_axis=0, tiled=True)  28.2 us
    all_gather x1, blocking collectives, body(): lax.all_gather(send_rows, 'req', axis=0, tiled=True)  23 us
    unnamed x48, local copies, waits for them, and re-layouts  22.3 us
    all_gather x1, waiting for transfers between devices, add_all(): pieces = lax.all_gather(value, name)  19.9 us
    scatter x1, local copies, waits for them, and re-layouts, body(): source_of = jnp.zeros((total_reqs,), jnp.int32).at[new_slot].set(everyone)  15.5 us
    dot_general x2, matrix products, bias_lookup(): jnp.einsum('rjk,kh->hrj', within.astype(jnp.float32), bias_table, precisi...  8.69 us
  transfers between devices with their start and end apart: 4, of which 3 were waited for; matrix products, arithmetic and copies ran while one was open for 15% of the time, Pallas kernels for 0%

profile of v1, /device:TPU:6, one launch (start us, length us, event | category | flops | bytes accessed | tf_op | source)
XLA Modules:
  0.0 334.7 jit_solution(240469363588978349)
XLA Ops:
  15.1 6.9 %fusion.8 = f32[2,256,512]{2,0,1:T(2,128)S(1)} fusion(s32[256,512]{1,0:T(8,128)S(1)} %subtract_clamp_fusion, s32[32]{0:T(128)S(1)} %pad_add_fusion, s32[32]{0:T(128)S(1)} %convert_reduce_fusion, f32[32,2]{0,1:T(2,128)} %param.27), kind=kOutput, calls=%fused_computation.35 | convolution fusion | flops 113246208 | bytes 1573376 | tf_op jit(solution)/shard_map/rjk,kh->hrj/dot_general | solution.py:26
  24.9 6.5 %fusion.89 = (bf16[1,256,64,128]{3,2,1,0:T(8,128)(2,1)}, bf16[1,256,64,128]{3,2,1,0:T(8,128)(2,1)}) fusion(bf16[2,256,64,128]{3,2,1,0:T(8,128)(2,1)} %param.22), kind=kLoop, calls=%fused_computation.187 | loop fusion | bytes 16777216 | tf_op jit(solution)/shard_map/slice | solution.py:64
  31.5 7.0 %copy.114 = bf16[1,256,64,128]{1,3,2,0:T(8,128)(2,1)} copy(bf16[1,256,64,128]{3,2,1,0:T(8,128)(2,1)} %get-tuple-element.12) | data formatting | bytes 8388608
  41.9 3.7 %multiply_reduce_fusion.1 = f32[2,256,64]{1,0,2:T(2,128)S(1)} fusion(bf16[2,256,64,64]{1,2,0,3:T(8,128)(2,1)} %bitcast.146, f32[2,256,64]{1,2,0:T(8,128)S(1)} %get-tuple-element.27), kind=kLoop, calls=%fused_computation.13 | loop fusion | flops 6258688 | bytes 4456448 | tf_op jit(solution)/shard_map/rhd,rthd->hrt/dot_general | solution.py:84
  47.5 2.2 fusion.5
  49.8 3.3 copy-done.1
  53.1 2.6 fusion.4
  57.0 6.9 %copy.116 = bf16[1,256,64,128]{1,3,2,0:T(8,128)(2,1)} copy(bf16[1,256,64,128]{3,2,1,0:T(8,128)(2,1)} %get-tuple-element.13) | data formatting | bytes 8388608
  66.0 2.3 copy.115
  68.2 3.1 multiply_reduce_fusion
  71.4 6.3 %fusion.19 = bf16[256,2,64]{0,2,1:T(8,128)(2,1)S(1)} fusion(f32[256,2,64]{0,2,1:T(8,128)S(1)} %multiply_reduce_fusion, f32[2,256,8,512]{3,1,2,0:T(8,128)} %copy-done.1, f32[2,256]{1,0:T(2,128)} %copy-done.12, f32[2,256]{1,0:T(2,128)} %copy-done.9, f32[2,256,512]{2,1,0:T(8,128)S(1)} %copy.78, pred[256,8,512]{2,0,1:T(8,128)(4,1)S(1)} %broadcast_and_fusion, ...), kind=kOutput, calls=%fused_computation.52 | convolution fusion | flops 281182208 | bytes 11802624 | tf_op jit(solution)/shard_map/hrgj,gjhd->rhd/dot_general | solution.py:98
  81.1 60.5 %all-reduce.2.cloned.1.call-done = f32[256,1024]{1,0:T(8,128)} async-done(((f32[256,1024]{1,0:T(8,128)}), f32[256,1024]{1,0:T(8,128)}) %all-reduce.2.cloned.1.call-update) | async-done | bytes 1048592 | tf_op jit(solution)/shard_map/psum | solution.py:149
  145.0 2.2 convolution_convert_fusion.1
  147.2 28.2 %all_to_all.10 = bf16[16,40,1024]{2,1,0:T(8,128)(2,1)S(1)} all-to-all(bf16[16,40,1024]{2,1,0:T(8,128)(2,1)S(1)} %bitcast.150), channel_id=1, replica_groups=mesh['req'=16,'tp'=8] {'req'}, dimensions={0} | all-to-all | bytes 2621440 | tf_op jit(solution)/shard_map/all_to_all | solution.py:177
  175.4 2.8 fusion.48
  178.2 4.4 %convolution_convert_fusion = bf16[640,1024]{1,0:T(8,128)(2,1)} fusion(bf16[640,1024]{1,0:T(8,128)(2,1)S(1)} %bitcast.152, f32[640,352]{0,1:T(8,128)} %fusion.48, bf16[1,352,1024]{2,1,0:T(8,128)(2,1)S(1)} %copy-done, bf16[1,1024,352]{1,2,0:T(8,128)(2,1)} %param.37), kind=kOutput, calls=%fused_computation.27 | convolution fusion | flops 925655040 | bytes 4964352 | tf_op jit(solution)/shard_map/dot_general | solution.py:183
  186.9 8.4 %broadcast_select_fusion = bf16[2,256,64,128]{3,2,1,0:T(8,128)(2,1)} fusion(bf16[2,256,64,128]{3,2,1,0:T(8,128)(2,1)} %param.22, pred[256,64]{1,0:T(8,128)(4,1)S(1)} %copy.89, bf16[2,256,128]{2,1,0:T(8,128)(2,1)S(1)} %copy.90), kind=kLoop, calls=%fused_computation.20 | loop fusion | flops 4194304 | bytes 16924672 | tf_op jit(solution)/shard_map/jit(_where)/select_n | solution.py:147
  195.3 4.8 %gather_fusion.3 = bf16[4,2,64,128]{3,2,1,0:T(8,128)(2,1)} fusion(bf16[2,256,64,128]{3,2,1,0:T(8,128)(2,1)} %broadcast_select_fusion, s32[1024]{0:T(1024)S(1)} %pad_clamp_fusion.3), kind=kCustom, calls=%fused_computation.4 | custom fusion | bytes 262160 | tf_op jit(solution)/shard_map/gather | solution.py:213
  200.4 15.5 %scatter_custom_fusion.1 = s32[4096]{0:T(1024)S(1)} fusion(s32[4096]{0:T(1024)S(1)} %add_select_fusion.1, s32[4096]{0:T(1024)S(1)} %iota.80, s32[]{:T(128)} %constant.37.clone.1), kind=kCustom, calls=%fused_computation.136 | custom fusion | bytes 16388 | tf_op jit(solution)/shard_map/scatter | solution.py:203
  216.5 19.9 %all-gather.8.cloned.1.call-done = bf16[5120,1024]{1,0:T(8,128)(2,1)} async-done(((bf16[640,1024]{1,0:T(8,128)(2,1)}), bf16[5120,1024]{1,0:T(8,128)(2,1)}) %all-gather.8.cloned.1.call-update) | async-done | bytes 10485776 | tf_op jit(solution)/shard_map/all_gather | solution.py:13
  236.4 8.1 %reduce_sum.124 = bf16[640,1024]{1,0:T(8,128)(2,1)} reduce(bf16[8,640,1024]{2,1,0:T(8,128)(2,1)} %bitcast.148, bf16[]{:T(256)} %constant.90.clone.1), dimensions={0}, to_apply=%region_15.16 | reduce | flops 4587520 | bytes 11796482 | tf_op jit(solution)/shard_map/reduce_sum | solution.py:14
  244.5 7.2 %all-to-all-start.1 = ((bf16[16,40,1024]{2,1,0:T(8,128)(2,1)}), bf16[16,40,1024]{2,1,0:T(8,128)(2,1)S(1)}, u32[]{:S(2)}, u32[]{:S(2)}) async-start(bf16[16,40,1024]{2,1,0:T(8,128)(2,1)} %bitcast.39), calls=%async_computation.1 | async-start | bytes 2621440 | tf_op jit(solution)/shard_map/all_to_all | solution.py:186
  252.8 44.5 %all-gather.6.cloned.1.call-done = bf16[64,2,64,128]{3,2,1,0:T(8,128)(2,1)} async-done(((bf16[4,2,64,128]{3,2,1,0:T(8,128)(2,1)}), bf16[64,2,64,128]{3,2,1,0:T(8,128)(2,1)}) %all-gather.6.cloned.1.call-update) | async-done | bytes 2097168 | tf_op jit(solution)/shard_map/all_gather | solution.py:216
  303.3 23.0 %all-gather.2 = bf16[16,4,1024]{2,1,0:T(4,128)(2,1)S(1)} all-gather(bf16[1,4,1024]{2,1,0:T(4,128)(2,1)S(1)} %bitcast.161), channel_id=3, replica_groups=mesh['req'=16,'tp'=8] {'req'}, dimensions={0}, use_global_device_ids=true | all-gather | bytes 139264 | tf_op jit(solution)/shard_map/all_gather | solution.py:215
  (130 shorter events, 40.1 us)
Async XLA Ops:
  7.2 171.1 %copy-start = (bf16[1,352,1024]{2,1,0:T(8,128)(2,1)S(1)}, bf16[1,352,1024]{2,1,0:T(8,128)(2,1)}, u32[]{:S(2)}) copy-start(bf16[1,352,1024]{2,1,0:T(8,128)(2,1)} %param.38) | copy-start | bytes 2162692
  7.2 134.4 %all-reduce.2.cloned.1.call-start = ((), (), s32[]{:S(2)}) async-start(), calls=%async_computation.2 | async-start | bytes 2097152 | tf_op jit(solution)/shard_map/psum | solution.py:149
  13.5 8.4 %copy-start.16 = (s32[32]{0:T(128)}, s32[32]{0:T(128)S(1)}, u32[]{:S(2)}) copy-start(s32[32]{0:T(128)S(1)} %convert_reduce_fusion) | copy-start | bytes 388
  15.0 6.9 %copy-start.20 = (s32[32]{0:T(128)}, s32[32]{0:T(128)S(1)}, u32[]{:S(2)}) copy-start(s32[32]{0:T(128)S(1)} %pad_add_fusion) | copy-start | bytes 388
  15.1 7.1 %copy-start.3 = (bf16[256,1024]{1,0:T(8,128)(2,1)S(1)}, bf16[256,1024]{1,0:T(8,128)(2,1)}, u32[]{:S(2)}) copy-start(bf16[256,1024]{1,0:T(8,128)(2,1)} %param.20) | copy-start | bytes 1572868
  15.1 7.3 %copy-start.2 = (bf16[2,8,512,128]{3,2,1,0:T(8,128)(2,1)S(1)}, bf16[2,8,512,128]{3,2,1,0:T(8,128)(2,1)}, u32[]{:S(2)}) copy-start(bf16[2,8,512,128]{3,2,1,0:T(8,128)(2,1)} %param.21) | copy-start | bytes 6291460
  22.4 16.1 %copy-start.15 = (f32[256]{0:T(256)}, f32[256]{0:T(256)S(1)}, u32[]{:S(2)}) copy-start(f32[256]{0:T(256)S(1)} %add_rsqrt_fusion.1) | copy-start | bytes 3076
  31.5 7.0 %copy-start.17 = (bf16[1024,128]{1,0:T(8,128)(2,1)S(1)}, bf16[1024,128]{1,0:T(8,128)(2,1)}, u32[]{:S(2)}) copy-start(bf16[1024,128]{1,0:T(8,128)(2,1)} %param.29) | copy-start | bytes 786436
  31.5 7.0 %copy-start.19 = (f32[1024]{0:T(1024)S(1)}, f32[1024]{0:T(1024)}, u32[]{:S(2)}) copy-start(f32[1024]{0:T(1024)} %param.28) | copy-start | bytes 12292
  31.5 7.4 %copy-start.18 = (bf16[1024,128]{1,0:T(8,128)(2,1)S(1)}, bf16[1024,128]{1,0:T(8,128)(2,1)}, u32[]{:S(2)}) copy-start(bf16[1024,128]{1,0:T(8,128)(2,1)} %param.30) | copy-start | bytes 786436
  31.5 9.1 %copy-start.14 = (f32[32,2]{0,1:T(2,128)S(1)}, f32[32,2]{0,1:T(2,128)}, u32[]{:S(2)}) copy-start(f32[32,2]{0,1:T(2,128)} %param.27) | copy-start | bytes 772
  38.5 9.0 %copy-start.4 = (bf16[1,8,512,128]{2,3,1,0:T(8,128)(2,1)S(1)}, bf16[1,8,512,128]{2,3,1,0:T(8,128)(2,1)}, u32[]{:S(2)}) copy-start(bf16[1,8,512,128]{2,3,1,0:T(8,128)(2,1)} %copy.113) | copy-start | bytes 3145732
  49.7 3.4 %copy-start.1 = (f32[2,256,8,512]{3,1,2,0:T(8,128)}, f32[2,256,8,512]{3,1,2,0:T(8,128)S(1)}, u32[]{:S(2)}) copy-start(f32[2,256,8,512]{3,1,2,0:T(8,128)S(1)} %get-tuple-element.26) | copy-start | bytes 25165828
  49.8 6.8 %copy-start.9 = (f32[2,256]{1,0:T(2,128)}, f32[2,256]{1,0:T(2,128)S(1)}, u32[]{:S(2)}) copy-start(f32[2,256]{1,0:T(2,128)S(1)} %maximum_maximum_fusion) | copy-start | bytes 6148
  71.4 6.3 %copy-start.6 = (bf16[128,1024]{1,0:T(8,128)(2,1)S(1)}, bf16[128,1024]{1,0:T(8,128)(2,1)}, u32[]{:S(2)}) copy-start(bf16[128,1024]{1,0:T(8,128)(2,1)} %param.32) | copy-start | bytes 786436
  71.4 7.7 %copy-start.11 = (s32[256,2]{0,1:T(2,128)S(1)}, s32[256,2]{0,1:T(2,128)}, u32[]{:S(2)}) copy-start(s32[256,2]{0,1:T(2,128)} %param.35) | copy-start | bytes 6148
  71.4 71.7 %copy-start.13 = (f32[1024]{0:T(1024)S(1)}, f32[1024]{0:T(1024)}, u32[]{:S(2)}) copy-start(f32[1024]{0:T(1024)} %param.33) | copy-start | bytes 12292
  79.0 157.4 %all-gather.8.cloned.1.call-start = ((), (), s32[]{:S(2)}) async-start(), calls=%async_computation.4 | async-start | bytes 11796480 | tf_op jit(solution)/shard_map/all_gather | solution.py:13
  145.0 37.7 %copy-start.7 = (s32[4096]{0:T(1024)S(1)}, s32[4096]{0:T(1024)}, u32[]{:S(2)}) copy-start(s32[4096]{0:T(1024)} %param.39) | copy-start | bytes 49156
  145.0 38.9 %copy-start.8 = (bf16[256,128]{0,1:T(8,128)(2,1)S(1)}, bf16[256,128]{0,1:T(8,128)(2,1)}, u32[]{:S(2)}) copy-start(bf16[256,128]{0,1:T(8,128)(2,1)} %convolution_convert_fusion.2) | copy-start | bytes 196612
  182.6 114.6 %all-gather.6.cloned.1.call-start = ((), (), s32[]{:S(2)}) async-start(), calls=%async_computation.3 | async-start | bytes 2228224 | tf_op jit(solution)/shard_map/all_gather | solution.py:216
  195.3 57.2 %copy-start.10 = (bf16[1024,16]{0,1:T(8,128)(2,1)S(1)}, bf16[1024,16]{0,1:T(8,128)(2,1)}, u32[]{:S(2)}) copy-start(bf16[1024,16]{0,1:T(8,128)(2,1)} %param.34) | copy-start | bytes 98308
  244.5 56.9 %all-to-all-start.1 = ((bf16[16,40,1024]{2,1,0:T(8,128)(2,1)}), bf16[16,40,1024]{2,1,0:T(8,128)(2,1)S(1)}, u32[]{:S(2)}, u32[]{:S(2)}) async-start(bf16[16,40,1024]{2,1,0:T(8,128)(2,1)} %bitcast.39), calls=%async_computation.1 | async-start | bytes 2621440 | tf_op jit(solution)/shard_map/all_to_all | solution.py:186
  327.4 0.8 copy-start.5
  (1 other events, 0.6 us)
Sparse Core Ops, SparseCore 0:
  79.1 62.3 all-reduce.1
  182.8 53.6 all-gather.7
  239.2 58.0 all-gather.5
